TPU v7x, 512 devices: a whole 4x4x16 slice. The times are simulated.
512 devices in a mesh: dp: 4 (over y), expert: 128 (over z, x, core).
Axes of the slice: x: 4, y: 4, z: 16, core: 2. Of those that a mesh axis runs over, the one named last changes fastest.
Arguments:
- grad_out: bfloat16 [16384, 4096], P(('dp', 'expert')), may hold values from -6 to 6
- expert_ids: int32 [16384, 8], P(('dp', 'expert')), may hold values from 0 to 127, all different within a row; in each aligned block of 32 rows (0 to 31, 32 to 63, ...) at most 2 rows name the same one
- route_weights: float32 [16384, 8], P(('dp', 'expert')), may hold values from 0.02 to 0.2
- hidden_act: bfloat16 [4, 128, 256, 1536], P('dp', 'expert'), may hold values from -6 to 6
- projection: bfloat16 [128, 1536, 256], P('expert', 'dp'), may hold values from -0.15625 to 0.15625
Outputs:
- projected_grad: bfloat16 [128, 4096, 256], P('expert', 'dp')
Inputs may be any that keep to these rules, and one draw needn't show every extreme that they name: `expert_ids`: each row names 8 different experts. Among the 32 tokens of one device (aligned blocks of rows), no expert is named more than 2 times, a bound that some block reaches.
All inputs are finite; a program needn't handle non-finite values.
Results may differ from a plain program's by a relative error of at most 0.0058.
Values may be sent and summed in bfloat16 or wider, within the bound.
No kernel may reach another device: no remote copies, remote signals or barrier semaphores. Data moves between devices by JAX's collectives and lax.ppermute only.
A program may use at most 64 MiB of HBM per device.

v0:
```python
import jax
import jax.numpy as jnp
from jax import lax
from jax.sharding import PartitionSpec as P


def shards(grad_out, expert_ids, route_weights, hidden_act, projection):
    token_count = grad_out.shape[0]
    width = grad_out.shape[1]
    top_count = expert_ids.shape[1]
    expert_count = lax.axis_size("expert")
    slot_count = hidden_act.shape[2]
    capacity = slot_count // expert_count
    route_total = token_count * top_count
    routed = expert_ids.reshape(-1)
    onehot = (routed[:, None] == jnp.arange(expert_count, dtype=jnp.int32)[None, :]).astype(
        jnp.int32
    )
    earlier = jnp.cumsum(onehot, axis=0) - onehot
    position = jnp.sum(earlier * onehot, axis=1)
    slot = routed * capacity + position
    table = jnp.full((expert_count * capacity,), -1, jnp.int32)
    table = table.at[slot].set(jnp.arange(route_total, dtype=jnp.int32))
    valid = table >= 0
    picked = jnp.maximum(table, 0)
    rows = grad_out[picked // top_count].astype(jnp.float32)
    weight = route_weights.reshape(-1)[picked]
    weighted = jnp.where(valid[:, None], weight[:, None] * rows, 0.0).astype(jnp.bfloat16)
    outgoing = weighted.reshape(expert_count, capacity, width)
    hidden = hidden_act[0, 0]
    reduced = jnp.dot(
        hidden,
        lax.all_gather(projection[0], "dp", axis=0, tiled=True),
        preferred_element_type=jnp.float32,
    ).astype(jnp.bfloat16)
    arrived = lax.all_to_all(outgoing, "expert", split_axis=0, concat_axis=0, tiled=True).reshape(
        slot_count, width
    )
    share = lax.psum_scatter(
        lax.dot_general(
            arrived, reduced, (((0,), (0,)), ((), ())), preferred_element_type=jnp.float32
        ),
        "dp",
        scatter_dimension=0,
        tiled=True,
    )
    return share.astype(jnp.bfloat16)[None]


def solution(mesh):
    in_specs = (
        P(("dp", "expert"), None),
        P(("dp", "expert"), None),
        P(("dp", "expert"), None),
        P("dp", "expert", None, None),
        P("expert", "dp", None),
    )
    out_specs = P("expert", "dp", None)
    return jax.shard_map(shards, mesh=mesh, in_specs=in_specs, out_specs=out_specs, check_vma=False)
```

profile of v0, /device:TPU:1, one launch (start us, length us, event | category | flops | bytes accessed | tf_op | source)
XLA Modules:
  0.0 209.0 jit_solution(662351124627535418)
XLA Ops:
  6.5 0.8 copy.7
  7.4 0.1 eq.29
  7.5 0.1 eq.25
  7.6 0.7 broadcast_multiply_fusion
  8.3 0.1 copy.9
  8.4 0.2 fusion.5
  8.7 0.1 copy.6
  8.8 0.1 mul.32
  8.8 0.2 fusion.7
  9.1 1.4 scatter_custom_fusion
  10.5 1.8 gather_fusion.1
  12.4 4.0 %reshape.71 = f32[128,2,4096]{2,1,0:T(2,128)} reshape(bf16[256,4096]{1,0:T(8,128)(2,1)S(1)} %gather_fusion.1) | data formatting | bytes 6291456 | tf_op jit(solution)/shard_map/convert_element_type | solution.py:26
  16.4 0.1 reshape.69
  16.5 1.9 gather_fusion
  18.5 0.1 mul.34
  18.6 0.2 broadcast_in_dim.31
  18.8 6.9 %select_convert_fusion = bf16[128,2,4096]{2,1,0:T(2,128)(2,1)} fusion(f32[128,2,4096]{2,1,0:T(2,128)} %reshape.71, pred[128,2]{1,0:T(8,128)(4,1)S(1)} %broadcast_in_dim.31, f32[128,2]{1,0:T(8,128)S(1)} %mul.34), kind=kLoop, calls=%fused_computation.3 | loop fusion | flops 3145728 | bytes 6292736 | tf_op jit(solution)/shard_map/convert_element_type | solution.py:28
  25.7 20.5 %all-to-all-start = ((bf16[128,2,4096]{2,1,0:T(2,128)(2,1)}), bf16[128,2,4096]{2,1,0:T(2,128)(2,1)S(1)}, u32[]{:S(2)}, u32[]{:S(2)}) async-start(bf16[128,2,4096]{2,1,0:T(2,128)(2,1)} %select_convert_fusion), calls=%async_computation | async-start | bytes 4194304 | tf_op jit(solution)/shard_map/all_to_all | solution.py:36
  46.3 13.2 %all-gather = bf16[1,1536,256]{2,1,0:T(8,128)(2,1)} all-gather(bf16[1,384,256]{2,1,0:T(8,128)(2,1)S(1)} %copy-done.2), channel_id=2, replica_groups=mesh['dp'=4,'expert'=128] {'dp'}, dimensions={1}, use_global_device_ids=true | all-gather | bytes 983040 | tf_op jit(solution)/shard_map/all_gather | solution.py:33
  59.5 82.7 %all-to-all-done = bf16[128,2,4096]{2,1,0:T(2,128)(2,1)S(1)} async-done(((bf16[128,2,4096]{2,1,0:T(2,128)(2,1)}), bf16[128,2,4096]{2,1,0:T(2,128)(2,1)S(1)}, u32[]{:S(2)}, u32[]{:S(2)}) %all-to-all-start) | async-done | bytes 2097184 | tf_op jit(solution)/shard_map/all_to_all | solution.py:36
  142.2 2.2 %reshape.70 = bf16[256,4096]{1,0:T(8,128)(2,1)} reshape(bf16[128,2,4096]{2,1,0:T(2,128)(2,1)S(1)} %all-to-all-done) | data formatting | bytes 4194304 | tf_op jit(solution)/shard_map/reshape | solution.py:36
  144.4 5.1 %fusion = f32[4096,256]{1,0:T(8,128)} fusion(bf16[256,4096]{1,0:T(8,128)(2,1)} %reshape.70, bf16[1,1536,256]{2,1,0:T(8,128)(2,1)} %all-gather, bf16[1,1,256,1536]{3,2,1,0:T(8,128)(2,1)S(1)} %copy-done), kind=kOutput, calls=%fused_computation.5 | convolution fusion | flops 738263040 | bytes 7864320 | tf_op jit(solution)/shard_map/dot_general | solution.py:40
  149.5 50.6 %reduce-scatter.2.cloned.1.call-done = f32[1024,256]{1,0:T(8,128)} async-done(((f32[4096,256]{1,0:T(8,128)}), f32[1024,256]{1,0:T(8,128)}) %reduce-scatter.2.cloned.1.call-update) | async-done | bytes 1048592 | tf_op jit(solution)/shard_map/reduce_scatter | solution.py:39
  200.1 2.1 convert_bitcast_fusion
  (22 shorter events, 0.3 us)
Async XLA Ops:
  6.5 137.9 %copy-start = (bf16[1,1,256,1536]{3,2,1,0:T(8,128)(2,1)S(1)}, bf16[1,1,256,1536]{3,2,1,0:T(8,128)(2,1)}, u32[]{:S(2)}) copy-start(bf16[1,1,256,1536]{3,2,1,0:T(8,128)(2,1)} %param.8) | copy-start | bytes 2359300
  6.5 4.0 %copy-start.1 = (bf16[32,4096]{1,0:T(8,128)(2,1)S(1)}, bf16[32,4096]{1,0:T(8,128)(2,1)}, u32[]{:S(2)}) copy-start(bf16[32,4096]{1,0:T(8,128)(2,1)} %param.5) | copy-start | bytes 786436
  12.4 4.0 %copy-start.3 = (f32[32,8]{0,1:T(8,128)S(1)}, f32[32,8]{0,1:T(8,128)}, u32[]{:S(2)}) copy-start(f32[32,8]{0,1:T(8,128)} %param.7) | copy-start | bytes 3076
  25.7 20.6 %copy-start.2 = (bf16[1,384,256]{2,1,0:T(8,128)(2,1)S(1)}, bf16[1,384,256]{2,1,0:T(8,128)(2,1)}, u32[]{:S(2)}) copy-start(bf16[1,384,256]{2,1,0:T(8,128)(2,1)} %param.9) | copy-start | bytes 589828
  25.7 116.4 %all-to-all-start = ((bf16[128,2,4096]{2,1,0:T(2,128)(2,1)}), bf16[128,2,4096]{2,1,0:T(2,128)(2,1)S(1)}, u32[]{:S(2)}, u32[]{:S(2)}) async-start(bf16[128,2,4096]{2,1,0:T(2,128)(2,1)} %select_convert_fusion), calls=%async_computation | async-start | bytes 4194304 | tf_op jit(solution)/shard_map/all_to_all | solution.py:36
  46.3 153.9 %reduce-scatter.2.cloned.1.call-start = ((), (), s32[]{:S(2)}) async-start(), calls=%async_computation.2 | async-start | bytes 5242880 | tf_op jit(solution)/shard_map/reduce_scatter | solution.py:39
Sparse Core Ops, SparseCore 0:
  149.7 50.4 reduce-scatter.1
where the time goes:
time: 209 us
  waiting for transfers between devices  133 us (64%)
  starting transfers between devices  20.6 us (10%)
  between operations  13.5 us (6%)
  local copies, waits for them, and re-layouts  13.2 us (6%)
  blocking collectives  13.2 us (6%)
  other arithmetic  10.2 us (5%)
  matrix products  5.11 us (2%)
    all_to_all x1, waiting for transfers between devices, shards(): lax.all_to_all(outgoing, 'expert', split_axis=0, concat_axis=0, tiled=True)  82.7 us
    reduce_scatter x1, waiting for transfers between devices, shards(): lax.psum_scatter(lax.dot_general(arrived, reduced, (((0,), (0,)), ((), ()...  50.6 us
    all_to_all x1, starting transfers between devices, shards(): lax.all_to_all(outgoing, 'expert', split_axis=0, concat_axis=0, tiled=True)  20.5 us
    all_gather x1, blocking collectives, shards(): lax.all_gather(projection[0], 'dp', axis=0, tiled=True)  13.2 us
    convert_element_type x1, other arithmetic, shards(): jnp.where(valid[:, None], weight[:, None] * rows, 0.0).astype(jnp.bfloat16)  6.93 us
    dot_general x1, matrix products, shards(): lax.dot_general(arrived, reduced, (((0,), (0,)), ((), ())), preferred_ele...  5.11 us
  transfers between devices with their start and end apart: 2, of which 2 were waited for; matrix products, arithmetic and copies ran while one was open for 0% of the time, Pallas kernels for 0%

commit v1 on v0

--- a/solution.py
+++ b/solution.py
@@ -30,7 +30,9 @@
     hidden = hidden_act[0, 0]
     reduced = jnp.dot(
         hidden,
-        lax.all_gather(projection[0], "dp", axis=0, tiled=True),
+        jnp.concatenate(
+            lax.all_to_all(jnp.stack([projection[0]] * lax.axis_size("dp"), 0), "dp", 0, 0), 0
+        ),
         preferred_element_type=jnp.float32,
     ).astype(jnp.bfloat16)
     arrived = lax.all_to_all(outgoing, "expert", split_axis=0, concat_axis=0, tiled=True).reshape(

time: 209 us -> 221 us (1.057)
  blocking collectives: 13.2 us -> 116 us
  waiting for transfers between devices: 133 us -> 58.9 us
  starting transfers between devices: 20.6 us -> 4.23 us
    all_to_all x0 -> x1, blocking collectives: none -> 116 us  [shards(): lax.all_to_all(outgoing, 'expert', split_axis=0, concat_axis=0, tiled=True)]
    all_to_all x1, waiting for transfers between devices: 82.7 us -> 6.45 us  [shards(): lax.all_to_all(jnp.stack([projection[0]] * lax.axis_size('dp'), 0), 'dp',...]
    all_to_all x1, starting transfers between devices: 20.5 us -> 4.19 us  [shards(): lax.all_to_all(jnp.stack([projection[0]] * lax.axis_size('dp'), 0), 'dp',...]
    all_gather x1 -> x0, blocking collectives: 13.2 us -> none  [shards(): lax.all_gather(projection[0], 'dp', axis=0, tiled=True)]
  transfers between devices with their start and end apart: 2 -> 2, of which waited for: 2 -> 2; matrix products, arithmetic and copies ran while one was open for 0% -> 1% of each run, Pallas kernels for 0% -> 0%
where the time goes in v1:
time: 221 us
  blocking collectives  116 us (52%)
  waiting for transfers between devices  58.9 us (27%)
  local copies, waits for them, and re-layouts  14.2 us (6%)
  between operations  13.5 us (6%)
  other arithmetic  8.82 us (4%)
  matrix products  5.11 us (2%)
  starting transfers between devices  4.23 us (2%)
    all_to_all x1, blocking collectives, shards(): lax.all_to_all(outgoing, 'expert', split_axis=0, concat_axis=0, tiled=True)  116 us
    reduce_scatter x1, waiting for transfers between devices, shards(): lax.psum_scatter(lax.dot_general(arrived, reduced, (((0,), (0,)), ((), ()...  52.4 us
    all_to_all x1, waiting for transfers between devices, shards(): lax.all_to_all(jnp.stack([projection[0]] * lax.axis_size('dp'), 0), 'dp',...  6.45 us
    convert_element_type x1, other arithmetic, shards(): jnp.where(valid[:, None], weight[:, None] * rows, 0.0).astype(jnp.bfloat16)  5.6 us
    dot_general x1, matrix products, shards(): lax.dot_general(arrived, reduced, (((0,), (0,)), ((), ())), preferred_ele...  5.11 us
  transfers between devices with their start and end apart: 2, of which 2 were waited for; matrix products, arithmetic and copies ran while one was open for 1% of the time, Pallas kernels for 0%

profile of v1, /device:TPU:1, one launch (start us, length us, event | category | flops | bytes accessed | tf_op | source)
XLA Modules:
  0.0 221.0 jit_solution(14695325288895301090)
XLA Ops:
  6.5 0.8 copy.7
  7.4 0.1 eq.29
  7.5 0.1 eq.25
  7.6 0.7 broadcast_multiply_fusion
  8.3 0.1 copy.9
  8.4 0.2 fusion.3
  8.8 0.1 mul.32
  8.8 0.2 fusion.5
  9.1 1.4 scatter_custom_fusion
  10.5 1.8 gather_fusion.1
  12.4 4.0 %reshape.76 = f32[128,2,4096]{2,1,0:T(2,128)} reshape(bf16[256,4096]{1,0:T(8,128)(2,1)S(1)} %gather_fusion.1) | data formatting | bytes 6291456 | tf_op jit(solution)/shard_map/convert_element_type | solution.py:26
  16.4 0.1 reshape.73
  16.5 1.9 gather_fusion
  18.5 0.1 mul.34
  18.6 0.2 broadcast_in_dim.31
  18.8 5.6 %select_convert_fusion = bf16[128,2,4096]{2,1,0:T(2,128)(2,1)S(1)} fusion(f32[128,2,4096]{2,1,0:T(2,128)} %reshape.76, pred[128,2]{1,0:T(8,128)(4,1)S(1)} %broadcast_in_dim.31, f32[128,2]{1,0:T(8,128)S(1)} %mul.34), kind=kLoop, calls=%fused_computation.3 | loop fusion | flops 3145728 | bytes 6292736 | tf_op jit(solution)/shard_map/convert_element_type | solution.py:28
  24.4 116.2 %all_to_all.10 = bf16[128,2,4096]{2,1,0:T(2,128)(2,1)S(1)} all-to-all(bf16[128,2,4096]{2,1,0:T(2,128)(2,1)S(1)} %select_convert_fusion), channel_id=1, replica_groups=mesh['dp'=4,'expert'=128] {'expert'}, dimensions={0} | all-to-all | bytes 4194304 | tf_op jit(solution)/shard_map/all_to_all | solution.py:38
  140.7 0.9 stack.3
  141.6 4.2 %all-to-all-start.1 = ((bf16[4,384,256]{2,1,0:T(8,128)(2,1)}), bf16[4,384,256]{2,1,0:T(8,128)(2,1)}, u32[]{:S(2)}, u32[]{:S(2)}) async-start(bf16[4,384,256]{2,1,0:T(8,128)(2,1)} %stack.3), calls=%async_computation.1 | async-start | bytes 1572864 | tf_op jit(solution)/shard_map/all_to_all | solution.py:34
  145.8 2.2 %reshape.74 = bf16[256,4096]{1,0:T(8,128)(2,1)} reshape(bf16[128,2,4096]{2,1,0:T(2,128)(2,1)S(1)} %all_to_all.10) | data formatting | bytes 4194304 | tf_op jit(solution)/shard_map/reshape | solution.py:38
  148.1 6.5 %all-to-all-done.1 = bf16[4,384,256]{2,1,0:T(8,128)(2,1)} async-done(((bf16[4,384,256]{2,1,0:T(8,128)(2,1)}), bf16[4,384,256]{2,1,0:T(8,128)(2,1)}, u32[]{:S(2)}, u32[]{:S(2)}) %all-to-all-start.1) | async-done | bytes 786464 | tf_op jit(solution)/shard_map/all_to_all | solution.py:34
  154.5 5.1 %fusion = f32[4096,256]{1,0:T(8,128)} fusion(bf16[256,4096]{1,0:T(8,128)(2,1)} %reshape.74, bf16[1536,256]{1,0:T(8,128)(2,1)} %bitcast.7, bf16[1,1,256,1536]{3,2,1,0:T(8,128)(2,1)S(1)} %copy-done), kind=kOutput, calls=%fused_computation.5 | convolution fusion | flops 738263040 | bytes 7864320 | tf_op jit(solution)/shard_map/dot_general | solution.py:42
  159.7 52.4 %reduce-scatter.2.cloned.1.call-done = f32[1024,256]{1,0:T(8,128)} async-done(((f32[4096,256]{1,0:T(8,128)}), f32[1024,256]{1,0:T(8,128)}) %reduce-scatter.2.cloned.1.call-update) | async-done | bytes 1048592 | tf_op jit(solution)/shard_map/reduce_scatter | solution.py:41
  212.1 2.1 convert_bitcast_fusion
  (23 shorter events, 0.3 us)
Async XLA Ops:
  6.5 148.0 %copy-start = (bf16[1,1,256,1536]{3,2,1,0:T(8,128)(2,1)S(1)}, bf16[1,1,256,1536]{3,2,1,0:T(8,128)(2,1)}, u32[]{:S(2)}) copy-start(bf16[1,1,256,1536]{3,2,1,0:T(8,128)(2,1)} %param.8) | copy-start | bytes 2359300
  6.5 4.0 %copy-start.1 = (bf16[32,4096]{1,0:T(8,128)(2,1)S(1)}, bf16[32,4096]{1,0:T(8,128)(2,1)}, u32[]{:S(2)}) copy-start(bf16[32,4096]{1,0:T(8,128)(2,1)} %param.5) | copy-start | bytes 786436
  12.4 4.0 %copy-start.3 = (f32[32,8]{0,1:T(8,128)S(1)}, f32[32,8]{0,1:T(8,128)}, u32[]{:S(2)}) copy-start(f32[32,8]{0,1:T(8,128)} %param.7) | copy-start | bytes 3076
  24.4 116.3 %copy-start.2 = (bf16[1,384,256]{2,1,0:T(8,128)(2,1)S(1)}, bf16[1,384,256]{2,1,0:T(8,128)(2,1)}, u32[]{:S(2)}) copy-start(bf16[1,384,256]{2,1,0:T(8,128)(2,1)} %param.9) | copy-start | bytes 589828
  141.6 13.0 %all-to-all-start.1 = ((bf16[4,384,256]{2,1,0:T(8,128)(2,1)}), bf16[4,384,256]{2,1,0:T(8,128)(2,1)}, u32[]{:S(2)}, u32[]{:S(2)}) async-start(bf16[4,384,256]{2,1,0:T(8,128)(2,1)} %stack.3), calls=%async_computation.1 | async-start | bytes 1572864 | tf_op jit(solution)/shard_map/all_to_all | solution.py:34
  145.8 66.3 %reduce-scatter.2.cloned.1.call-start = ((), (), s32[]{:S(2)}) async-start(), calls=%async_computation.3 | async-start | bytes 5242880 | tf_op jit(solution)/shard_map/reduce_scatter | solution.py:41
Sparse Core Ops, SparseCore 0:
  159.8 52.2 reduce-scatter.1
